TPU v7x, 32 devices: a whole 2x2x4 slice. The times are simulated.
32 devices in a mesh: shot: 4 (over x, core), band: 4 (over z), net: 2 (over y).
Axes of the slice: x: 2, y: 2, z: 4, core: 2. Of those that a mesh axis runs over, the one named last changes fastest.
Arguments:
- velocity: float32 [128, 1024], P('band'), may hold values from 1.5 to 4
- wave_now: float32 [16, 128, 1024], P(('shot', 'net'), 'band'), may hold values from -6 to 6
- wave_before: float32 [16, 128, 1024], P(('shot', 'net'), 'band'), may hold values from -6 to 6
- adjoint_last: float32 [16, 128, 1024], P(('shot', 'net'), 'band'), may hold values from -6 to 6
- adjoint_after: float32 [16, 128, 1024], P(('shot', 'net'), 'band'), may hold values from -6 to 6
- wavelet: float32 [16, 16], P(('shot', 'net')), may hold values from -72 to 72
- source_col: int32 [16], P(('shot', 'net')), may hold values from 0 to 1023
- rec_first: int32 [16], P(('shot', 'net')), may hold values from 0 to 1022
- rec_last: int32 [16], P(('shot', 'net')), may hold values from 1 to 1023
- rec_count: int32 [16], P(('shot', 'net')), may hold values from 2 to 128, as said below
- observed: float32 [16, 16, 128], P(('shot', 'net')), may hold values from -72 to 72
- conv_in: float32 [32, 18], replicated, may hold values from -1.5 to 1.5
- conv_mid: float32 [32, 288], replicated, may hold values from -0.375 to 0.375
- conv_out: float32 [1, 288], replicated, may hold values from -0.375 to 0.375
- cotangent: float32 [128, 1024], P('band', ('shot', 'net')), may hold values from -0.06629126 to 0.06629126
Outputs:
- new_velocity: float32 [128, 1024], P('band', ('shot', 'net'))
- grad_in: float32 [32, 18], replicated
- grad_mid: float32 [32, 288], replicated
- grad_out: float32 [1, 288], replicated
Inputs may be any that keep to these rules, and one draw needn't show every extreme that they name: rec_last - rec_first >= rec_count - 1 for every shot; some shot has 128 receivers.
All inputs are finite; a program needn't handle non-finite values.
Results may differ from a plain program's by a relative error of at most 0.0003.
Values sent between devices are 32-bit elements; how exact they have to be, the bound alone decides.
A program may use at most 128 MiB of HBM per device.

v0:
```python
import jax
import jax.numpy as jnp
from jax import lax
from jax.sharding import PartitionSpec as P

coefficients = (-205.0 / 72.0, 8.0 / 5.0, -1.0 / 5.0, 8.0 / 315.0, -1.0 / 560.0)
speed_factor = 0.11
source_depth = 2
receiver_depth = 3
highest = lax.Precision.HIGHEST


def extended_2(block, sides, width):
    for axis, dim in sides:
        count = lax.axis_size(axis)
        forward = [(i, i + 1) for i in range(count - 1)]
        backward = [(target, source) for source, target in forward]
        low = lax.ppermute(
            lax.slice_in_dim(block, block.shape[dim] - width, None, axis=dim), axis, forward
        )
        high = lax.ppermute(lax.slice_in_dim(block, 0, width, axis=dim), axis, backward)
        block = jnp.concatenate([low, block, high], axis=dim)
    return block


def laplace(extended):
    middle = extended[..., 4:-4, :]
    height = middle.shape[-2]
    breadth = middle.shape[-1]
    padding = [(0, 0)] * (middle.ndim - 1) + [(4, 4)]
    padded = jnp.pad(middle, padding)
    running = 2.0 * coefficients[0] * middle
    for reach in range(1, 5):
        vertical = (
            extended[..., 4 - reach : 4 - reach + height, :]
            + extended[..., 4 + reach : 4 + reach + height, :]
        )
        lateral = (
            padded[..., 4 - reach : 4 - reach + breadth]
            + padded[..., 4 + reach : 4 + reach + breadth]
        )
        running = running + coefficients[reach] * (vertical + lateral)
    return running


def receiver_table(rec_first, rec_last, rec_count, breadth, slots):
    columns = jnp.arange(breadth, dtype=jnp.int32)
    slot_ids = jnp.arange(slots, dtype=jnp.int32)
    placed = (
        rec_first[:, None]
        + slot_ids[None, :] * (rec_last - rec_first)[:, None] // (rec_count - 1)[:, None]
    )
    active = slot_ids[None, :] < rec_count[:, None]
    return ((columns[None, :, None] == placed[:, None, :]) & active[:, None, :]).astype(jnp.float32)


def patches(extended, height, breadth):
    parts = [
        extended[:, down : down + height, across : across + breadth]
        for down in range(3)
        for across in range(3)
    ]
    return jnp.concatenate(parts, 0).reshape(-1, height * breadth)


def flipped(weights):
    outputs = weights.shape[0]
    channels = weights.shape[1] // 9
    return (
        weights.reshape(outputs, 9, channels)[:, ::-1, :]
        .transpose(2, 1, 0)
        .reshape(channels, 9 * outputs)
    )


def sigmoid_slope(values):
    squashed = jax.nn.sigmoid(values)
    return squashed * (1.0 + values * (1.0 - squashed))


def matmul(left, right):
    return jnp.dot(left, right, precision=highest)


def outer_sum(left, right):
    return lax.dot_general(left, right, (((1,), (1,)), ((), ())), precision=highest)


def on_device(
    velocity,
    wave_now,
    wave_before,
    adjoint_last,
    adjoint_after,
    wavelet,
    source_col,
    rec_first,
    rec_last,
    rec_count,
    observed,
    conv_in,
    conv_mid,
    conv_out,
    cotangent,
):
    rows_here = velocity.shape[0]
    breadth = velocity.shape[1]
    shot_here = wave_now.shape[0]
    num_steps = wavelet.shape[1]
    slots = observed.shape[2]
    piece_cols = cotangent.shape[1]
    first_row = lax.axis_index("band") * rows_here
    speed_sq = (velocity * speed_factor) ** 2
    columns = jnp.arange(breadth, dtype=jnp.int32)
    source_cols = (columns[None, :] == source_col[:, None]).astype(jnp.float32)[:, None, :]
    table = receiver_table(rec_first, rec_last, rec_count, breadth, slots)
    active = (jnp.arange(slots, dtype=jnp.int32)[None, :] < rec_count[:, None]).astype(jnp.float32)

    def source_term(row_start, height, amount):
        row_ids = row_start + jnp.arange(height, dtype=jnp.int32)
        marked = (row_ids == source_depth).astype(jnp.float32)[None, :, None]
        return marked * source_cols * amount[:, None, None]

    def receiver_term(row_start, height, residual):
        row_ids = row_start + jnp.arange(height, dtype=jnp.int32)
        marked = (row_ids == receiver_depth).astype(jnp.float32)[None, :, None]
        injected = jnp.einsum("swk,sk->sw", table, residual, precision=highest)
        return marked * injected[:, None, :]

    speed_wide = extended_2(speed_sq, (("band", 0),), 16)

    def propagate(start, prior, drive, inject):
        grouped = drive.reshape((num_steps // 4, 4) + drive.shape[1:])

        def block(carry, amounts):
            stacked = extended_2(jnp.stack([carry[0], carry[1]]), (("band", 2),), 16)
            current = stacked[0]
            earlier = stacked[1]
            margin = 16
            saved = []
            for offset in range(4):
                inner = margin - 4
                speed_part = speed_wide[16 - inner : 16 + rows_here + inner]
                fresh = (
                    2.0 * current[:, 4:-4]
                    - earlier[:, 4:-4]
                    + speed_part * laplace(current)
                    + inject(first_row - inner, rows_here + 2 * inner, amounts[offset])
                )
                earlier = current[:, 4:-4]
                current = fresh
                margin = inner
                saved.append(fresh[:, inner : inner + rows_here])
            return ((current, earlier), jnp.stack(saved))

        ignored, states = lax.scan(block, (start, prior), grouped)
        return states.reshape((num_steps,) + start.shape)

    stored = propagate(wave_now, wave_before, wavelet.T, source_term)
    samples = jnp.einsum("tsw,swk->tsk", stored[:, :, receiver_depth, :], table, precision=highest)
    misfit = (samples - jnp.transpose(observed, (1, 0, 2))) * active[None]
    adjoint = propagate(adjoint_last, adjoint_after, misfit[::-1], receiver_term)
    imaging = jnp.sum(stored * adjoint[::-1], axis=(0, 1))
    group_count = shot_here * lax.axis_size(("shot", "net"))
    start_col = lax.axis_index(("shot", "net")) * piece_cols
    gathered = lax.psum(imaging, ("shot", "net"))
    summed = lax.dynamic_slice_in_dim(gathered, start_col, piece_cols, 1)
    scaled = summed / float(num_steps * group_count) ** 0.5
    velocity_piece = lax.dynamic_slice_in_dim(velocity, start_col, piece_cols, 1)

    def spread(field):
        extended = extended_2(field, (("band", 1), (("shot", "net"), 2)), 1)
        return patches(extended, rows_here, piece_cols)

    layer_zero = spread(jnp.stack([velocity_piece, scaled]))
    before_one = matmul(conv_in, layer_zero)
    hidden_one = jax.nn.silu(before_one)
    layer_one = spread(hidden_one.reshape(-1, rows_here, piece_cols))
    before_two = matmul(conv_mid, layer_one)
    hidden_two = jax.nn.silu(before_two)
    layer_two = spread(hidden_two.reshape(-1, rows_here, piece_cols))
    update = matmul(conv_out, layer_two).reshape(rows_here, piece_cols)
    new_velocity = velocity_piece + update
    grad_out = outer_sum(cotangent.reshape(1, -1), layer_two)
    slope_two = matmul(flipped(conv_out), spread(cotangent[None])) * sigmoid_slope(before_two)
    grad_mid = outer_sum(slope_two, layer_one)
    slope_one = matmul(
        flipped(conv_mid), spread(slope_two.reshape(-1, rows_here, piece_cols))
    ) * sigmoid_slope(before_one)
    grad_in = outer_sum(slope_one, layer_zero)
    totals = lax.psum((grad_in, grad_mid, grad_out), ("shot", "band", "net"))
    return (new_velocity, totals[0], totals[1], totals[2])


def solution(mesh):
    in_specs = (
        P("band", None),
        P(("shot", "net"), "band", None),
        P(("shot", "net"), "band", None),
        P(("shot", "net"), "band", None),
        P(("shot", "net"), "band", None),
        P(("shot", "net"), None),
        P(("shot", "net")),
        P(("shot", "net")),
        P(("shot", "net")),
        P(("shot", "net")),
        P(("shot", "net"), None, None),
        P(),
        P(),
        P(),
        P("band", ("shot", "net")),
    )
    out_specs = (P("band", ("shot", "net")), P(), P(), P())
    return jax.shard_map(
        on_device, mesh=mesh, in_specs=in_specs, out_specs=out_specs, check_vma=False
    )
```

profile of v0, /device:TPU:0, one launch (start us, length us, event | category | flops | bytes accessed | tf_op | source)
XLA Modules:
  0.0 534.4 jit_solution(12603834938900833449)
XLA Ops:
  8.0 4.9 collective-permute-start.18
  15.2 4.5 collective-permute-start.4
  31.4 4.5 collective-permute-start.20
  40.0 62.5 %while.34 = (s32[]{:T(128)}, f32[2,32,1024]{2,1,0:T(8,128)S(1)}, f32[2,32,1024]{2,1,0:T(8,128)S(1)}, f32[4,4,2,32,1024]{4,3,2,1,0:T(8,128)}, f32[64,1024]{1,0:T(...) while((s32[]{:T(128)}, f32[2,32,1024]{2,1,0:T(8,128)S(1)}, ...), condition=%wide.region_1.2_spmd.clone, body=%wide.region_0.1_spmd.clone.sunk | while | flops 11801106 | bytes 31434516 | solution.py:156
  41.3 5.2 collective-permute-start.1
  46.7 3.9 collective-permute-done
  58.0 5.0 collective-permute-start.1
  73.7 5.0 collective-permute-start.1
  88.8 5.0 collective-permute-start.1
  102.5 4.6 copy.175
  110.2 61.6 %while.35 = (s32[]{:T(128)}, f32[2,32,1024]{2,1,0:T(8,128)S(1)}, f32[2,32,1024]{2,1,0:T(8,128)S(1)}, f32[4,4,2,32,1024]{4,3,2,1,0:T(8,128)}, f32[64,1024]{1,0:T(...) while((s32[]{:T(128)}, f32[2,32,1024]{2,1,0:T(8,128)S(1)}, ...), condition=%wide.region_3.4_spmd.clone, body=%wide.region_2.3_spmd.clone.sunk | while | flops 27165204 | bytes 31534800 | solution.py:156
  112.0 5.0 collective-permute-start.3
  127.6 4.6 collective-permute-start.3
  142.8 4.6 collective-permute-start.3
  158.0 4.6 collective-permute-start.3
  171.8 6.6 %copy.176 = f32[16,2,32,1024]{3,0,1,2:T(8,128)} copy(f32[16,2,32,1024]{3,2,1,0:T(8,128)} %bitcast.368) | data formatting | bytes 8388608 | tf_op jit(solution)/shard_map/reshape | solution.py:157
  178.4 6.8 %rev.13 = f32[16,2,32,1024]{3,0,1,2:T(8,128)} reverse(f32[16,2,32,1024]{3,0,1,2:T(8,128)} %copy.176), dimensions={0} | reverse | bytes 8388608 | tf_op jit(solution)/shard_map/rev | solution.py:163
  185.3 7.0 %multiply_reduce_fusion = f32[32,1024]{1,0:T(8,128)} fusion(f32[16,2,32,1024]{3,0,1,2:T(8,128)} %rev.13, f32[16,2,32,1024]{3,2,1,0:T(8,128)} %bitcast.367), kind=kLoop, calls=%fused_computation.332 | loop fusion | flops 2064384 | bytes 8519680 | tf_op jit(solution)/shard_map/reduce_sum | solution.py:163
  192.4 55.1 %all-reduce.11.cloned.1.call-done = f32[32,1024]{1,0:T(8,128)} async-done(((f32[32,1024]{1,0:T(8,128)}), f32[32,1024]{1,0:T(8,128)}) %all-reduce.11.cloned.1.call-update) | async-done | bytes 131088 | tf_op jit(solution)/shard_map/psum | solution.py:166
  258.5 4.5 collective-permute-start.8
  268.2 5.1 collective-permute-start.10
  276.8 3.6 copy.125
  285.7 5.3 collective-permute-start.12
  293.0 4.4 pad_maximum_fusion.4
  297.5 3.7 fusion.218
  301.2 3.5 copy.135
  311.6 3.8 fusion.219
  315.3 3.6 copy.133
  336.8 4.7 fusion.230
  344.4 5.1 collective-permute-start.14
  357.2 5.1 collective-permute-start.22
  362.3 3.6 copy.138
  371.7 5.1 collective-permute-start.16
  376.8 3.6 copy.151
  380.4 3.6 copy.153
  386.5 5.0 collective-permute-start.24
  395.2 3.6 pad_maximum_fusion.6
  411.0 7.1 %pad_maximum_fusion.5 = (f32[32,34,129]{1,0,2:T(8,128)S(1)}, f32[32,34,129]{1,0,2:T(8,128)S(1)}) fusion(f32[32,34,1]{1,0,2:T(8,128)} %collective-permute-done.17, f32[32,1,128]{1,0,2:T(8,128)} %copy.140, f32[32,32,128]{1,0,2:T(8,128)} %copy-done.6, f32[32,1,128]{1,0,2:T(8,128)} %copy.138, f32[32,34,1]{1,0,2:T(8,128)} %collective-permute-done.16), kind=kLoop, calls=%fused_computation.336 | loop fusion | flops 842112 | bytes 1688576 | tf_op jit(solution)/shard_map/concatenate | solution.py:22
  418.1 3.9 fusion.216
  425.4 3.6 copy.145
  432.5 6.7 %fusion.215 = (f32[32,32,128]{1,0,2:T(8,128)}, f32[32,32,128]{1,0,2:T(8,128)}, f32[32,32,128]{1,0,2:T(8,128)}) fusion(f32[32,34,129]{1,0,2:T(8,128)} %get-tuple-element.522), kind=kLoop, calls=%fused_computation.439 | loop fusion | bytes 3145728 | tf_op jit(solution)/shard_map/slice | solution.py:59
  442.7 3.5 copy.157
  446.3 3.5 copy.154
  461.3 3.8 fusion.217
  465.1 3.6 copy.146
  468.7 3.5 copy.144
  483.0 3.8 fusion.231
  488.1 39.2 %all-reduce.8 = (f32[32,18]{0,1:T(8,128)}, f32[32,288]{1,0:T(8,128)}, f32[1,288]{1,0:T(1,128)}) all-reduce(f32[32,18]{0,1:T(8,128)S(1)} %copy-done.41, f32[32,288]{1,0:T(8,128)S(1)} %copy-done.38, f32[1,288]{1,0:T(1,128)S(1)} %fusion.231), channel_id=1, replica_groups=mesh['shot'=4,'band'=4,'net'=2] {'shot','band','net'}, use_global_device_ids=true, to_apply=%region_6.7 | all-reduce | flops 10080 | bytes 80640 | tf_op jit(solution)/shard_map/psum | solution.py:191
  (471 shorter events, 220.8 us)
Async XLA Ops:
  7.2 258.2 %copy-start = (f32[32,18]{0,1:T(8,128)S(1)}, f32[32,18]{0,1:T(8,128)}, u32[]{:S(2)}) copy-start(f32[32,18]{0,1:T(8,128)} %param.30) | copy-start | bytes 6916
  7.2 32.8 %copy-start.3 = (f32[2,32,1024]{2,1,0:T(8,128)S(1)}, f32[2,32,1024]{2,1,0:T(8,128)}, u32[]{:S(2)}) copy-start(f32[2,32,1024]{2,1,0:T(8,128)} %param.20) | copy-start | bytes 786436
  7.2 32.8 %copy-start.4 = (f32[2,32,1024]{2,1,0:T(8,128)S(1)}, f32[2,32,1024]{2,1,0:T(8,128)}, u32[]{:S(2)}) copy-start(f32[2,32,1024]{2,1,0:T(8,128)} %param.21) | copy-start | bytes 786436
  7.2 32.8 %copy-start.42 = (s32[2]{0:T(128)S(1)}, s32[2]{0:T(128)}, u32[]{:S(2)}) copy-start(s32[2]{0:T(128)} %param.25) | copy-start | bytes 28
  7.2 240.3 %all-reduce.11.cloned.1.call-start = ((), (), s32[]{:S(2)}) async-start(), calls=%async_computation | async-start | bytes 262144 | tf_op jit(solution)/shard_map/psum | solution.py:166
  8.0 21.3 %collective-permute-start.18 = (f32[1,1,128]{2,1,0:T(1,128)S(1)}, f32[1,1,128]{2,1,0:T(1,128)S(1)}, u32[]{:S(2)}, u32[]{:S(2)}) collective-permute-start(f32[1,1,128]{2,1,0:T(1,128)S(1)} %get-tuple-element.591), channel_id=1, source_target_pairs={{0,2},{2,4},{4,6},{1,3},{3,5},{5,7},{8,10},{10,12},{12,14},{9,11},... | collective-permute-start | bytes 1544 | tf_op jit(solution)/shard_map/ppermute | solution.py:18
  13.0 16.3 %collective-permute-start.19 = (f32[1,1,128]{2,1,0:T(1,128)S(1)}, f32[1,1,128]{2,1,0:T(1,128)S(1)}, u32[]{:S(2)}, u32[]{:S(2)}) collective-permute-start(f32[1,1,128]{2,1,0:T(1,128)S(1)} %get-tuple-element.592), channel_id=1, source_target_pairs={{2,0},{4,2},{6,4},{3,1},{5,3},{7,5},{10,8},{12,10},{14,12},{11,9},... | collective-permute-start | bytes 1544 | tf_op jit(solution)/shard_map/ppermute | solution.py:21
  15.2 22.1 %collective-permute-start.4 = (f32[16,1024]{1,0:T(8,128)S(1)}, f32[16,1024]{1,0:T(8,128)S(1)}, u32[]{:S(2)}, u32[]{:S(2)}) collective-permute-start(f32[16,1024]{1,0:T(8,128)S(1)} %get-tuple-element.563), channel_id=1, source_target_pairs={{0,2},{2,4},{4,6},{1,3},{3,5},{5,7},{8,10},{10,12},{12,14},{9,11},... | collective-permute-start | bytes 196616 | tf_op jit(solution)/shard_map/ppermute | solution.py:18
  19.8 17.6 %collective-permute-start.5 = (f32[16,1024]{1,0:T(8,128)S(1)}, f32[16,1024]{1,0:T(8,128)S(1)}, u32[]{:S(2)}, u32[]{:S(2)}) collective-permute-start(f32[16,1024]{1,0:T(8,128)S(1)} %get-tuple-element.564), channel_id=1, source_target_pairs={{2,0},{4,2},{6,4},{3,1},{5,3},{7,5},{10,8},{12,10},{14,12},{11,9},... | collective-permute-start | bytes 196616 | tf_op jit(solution)/shard_map/ppermute | solution.py:21
  30.1 162.2 %collective-permute-start.21 = (f32[1,34,1]{2,1,0:T(8,128)S(1)}, f32[1,34,1]{2,1,0:T(8,128)S(1)}, u32[]{:S(2)}, u32[]{:S(2)}) collective-permute-start(f32[1,34,1]{2,1,0:T(8,128)S(1)} %get-tuple-element.585), channel_id=1, source_target_pairs={{1,0},{8,1},{9,8},{16,9},{17,16},{24,17},{25,24},{3,2},{10,3},{11,... | collective-permute-start | bytes 416 | tf_op jit(solution)/shard_map/ppermute | solution.py:21
  31.4 161.0 %collective-permute-start.20 = (f32[1,34,1]{2,1,0:T(8,128)S(1)}, f32[1,34,1]{2,1,0:T(8,128)S(1)}, u32[]{:S(2)}, u32[]{:S(2)}) collective-permute-start(f32[1,34,1]{2,1,0:T(8,128)S(1)} %get-tuple-element.586), channel_id=1, source_target_pairs={{0,1},{1,8},{8,9},{9,16},{16,17},{17,24},{24,25},{2,3},{3,10},{10,... | collective-permute-start | bytes 416 | tf_op jit(solution)/shard_map/ppermute | solution.py:18
  40.0 10.6 %collective-permute-start = (f32[2,2,16,1024]{3,2,1,0:T(8,128)S(1)}, f32[2,2,16,1024]{3,2,1,0:T(8,128)S(1)}, u32[]{:S(2)}, u32[]{:S(2)}) collective-permute-start(f32[2,2,16,1024]{3,2,1,0:T(8,128)S(1)} %get-tuple-element.760), channel_id=1, source_target_pairs={{2,0},{4,2},{6,4},{3,1},{5,3},{7,5},{10,8},{12,10},{14,12},{11,9},... | collective-permute-start | bytes 786440 | tf_op jit(solution)/shard_map/while/body/eval_jaxpr/ppermute | solution.py:21
  41.3 10.5 %collective-permute-start.1 = (f32[2,2,16,1024]{3,2,1,0:T(8,128)S(1)}, f32[2,2,16,1024]{3,2,1,0:T(8,128)S(1)}, u32[]{:S(2)}, u32[]{:S(2)}) collective-permute-start(f32[2,2,16,1024]{3,2,1,0:T(8,128)S(1)} %get-tuple-element.761), channel_id=1, source_target_pairs={{0,2},{2,4},{4,6},{1,3},{3,5},{5,7},{8,10},{10,12},{12,14},{9,11},... | collective-permute-start | bytes 786440 | tf_op jit(solution)/shard_map/while/body/eval_jaxpr/ppermute | solution.py:18
  56.7 9.6 %collective-permute-start = (f32[2,2,16,1024]{3,2,1,0:T(8,128)S(1)}, f32[2,2,16,1024]{3,2,1,0:T(8,128)S(1)}, u32[]{:S(2)}, u32[]{:S(2)}) collective-permute-start(f32[2,2,16,1024]{3,2,1,0:T(8,128)S(1)} %get-tuple-element.760), channel_id=1, source_target_pairs={{2,0},{4,2},{6,4},{3,1},{5,3},{7,5},{10,8},{12,10},{14,12},{11,9},... | collective-permute-start | bytes 786440 | tf_op jit(solution)/shard_map/while/body/eval_jaxpr/ppermute | solution.py:21
  58.0 9.5 %collective-permute-start.1 = (f32[2,2,16,1024]{3,2,1,0:T(8,128)S(1)}, f32[2,2,16,1024]{3,2,1,0:T(8,128)S(1)}, u32[]{:S(2)}, u32[]{:S(2)}) collective-permute-start(f32[2,2,16,1024]{3,2,1,0:T(8,128)S(1)} %get-tuple-element.761), channel_id=1, source_target_pairs={{0,2},{2,4},{4,6},{1,3},{3,5},{5,7},{8,10},{10,12},{12,14},{9,11},... | collective-permute-start | bytes 786440 | tf_op jit(solution)/shard_map/while/body/eval_jaxpr/ppermute | solution.py:18
  72.4 8.8 %collective-permute-start = (f32[2,2,16,1024]{3,2,1,0:T(8,128)S(1)}, f32[2,2,16,1024]{3,2,1,0:T(8,128)S(1)}, u32[]{:S(2)}, u32[]{:S(2)}) collective-permute-start(f32[2,2,16,1024]{3,2,1,0:T(8,128)S(1)} %get-tuple-element.760), channel_id=1, source_target_pairs={{2,0},{4,2},{6,4},{3,1},{5,3},{7,5},{10,8},{12,10},{14,12},{11,9},... | collective-permute-start | bytes 786440 | tf_op jit(solution)/shard_map/while/body/eval_jaxpr/ppermute | solution.py:21
  73.7 8.9 %collective-permute-start.1 = (f32[2,2,16,1024]{3,2,1,0:T(8,128)S(1)}, f32[2,2,16,1024]{3,2,1,0:T(8,128)S(1)}, u32[]{:S(2)}, u32[]{:S(2)}) collective-permute-start(f32[2,2,16,1024]{3,2,1,0:T(8,128)S(1)} %get-tuple-element.761), channel_id=1, source_target_pairs={{0,2},{2,4},{4,6},{1,3},{3,5},{5,7},{8,10},{10,12},{12,14},{9,11},... | collective-permute-start | bytes 786440 | tf_op jit(solution)/shard_map/while/body/eval_jaxpr/ppermute | solution.py:18
  87.5 8.7 %collective-permute-start = (f32[2,2,16,1024]{3,2,1,0:T(8,128)S(1)}, f32[2,2,16,1024]{3,2,1,0:T(8,128)S(1)}, u32[]{:S(2)}, u32[]{:S(2)}) collective-permute-start(f32[2,2,16,1024]{3,2,1,0:T(8,128)S(1)} %get-tuple-element.760), channel_id=1, source_target_pairs={{2,0},{4,2},{6,4},{3,1},{5,3},{7,5},{10,8},{12,10},{14,12},{11,9},... | collective-permute-start | bytes 786440 | tf_op jit(solution)/shard_map/while/body/eval_jaxpr/ppermute | solution.py:21
  88.8 8.9 %collective-permute-start.1 = (f32[2,2,16,1024]{3,2,1,0:T(8,128)S(1)}, f32[2,2,16,1024]{3,2,1,0:T(8,128)S(1)}, u32[]{:S(2)}, u32[]{:S(2)}) collective-permute-start(f32[2,2,16,1024]{3,2,1,0:T(8,128)S(1)} %get-tuple-element.761), channel_id=1, source_target_pairs={{0,2},{2,4},{4,6},{1,3},{3,5},{5,7},{8,10},{10,12},{12,14},{9,11},... | collective-permute-start | bytes 786440 | tf_op jit(solution)/shard_map/while/body/eval_jaxpr/ppermute | solution.py:18
  110.7 10.7 %collective-permute-start.2 = (f32[2,2,16,1024]{3,2,1,0:T(8,128)S(1)}, f32[2,2,16,1024]{3,2,1,0:T(8,128)S(1)}, u32[]{:S(2)}, u32[]{:S(2)}) collective-permute-start(f32[2,2,16,1024]{3,2,1,0:T(8,128)S(1)} %get-tuple-element.783), channel_id=1, source_target_pairs={{2,0},{4,2},{6,4},{3,1},{5,3},{7,5},{10,8},{12,10},{14,12},{11,9},... | collective-permute-start | bytes 786440 | tf_op jit(solution)/shard_map/while/body/eval_jaxpr/ppermute | solution.py:21
  112.0 9.5 %collective-permute-start.3 = (f32[2,2,16,1024]{3,2,1,0:T(8,128)S(1)}, f32[2,2,16,1024]{3,2,1,0:T(8,128)S(1)}, u32[]{:S(2)}, u32[]{:S(2)}) collective-permute-start(f32[2,2,16,1024]{3,2,1,0:T(8,128)S(1)} %get-tuple-element.784), channel_id=1, source_target_pairs={{0,2},{2,4},{4,6},{1,3},{3,5},{5,7},{8,10},{10,12},{12,14},{9,11},... | collective-permute-start | bytes 786440 | tf_op jit(solution)/shard_map/while/body/eval_jaxpr/ppermute | solution.py:18
  126.3 10.3 %collective-permute-start.2 = (f32[2,2,16,1024]{3,2,1,0:T(8,128)S(1)}, f32[2,2,16,1024]{3,2,1,0:T(8,128)S(1)}, u32[]{:S(2)}, u32[]{:S(2)}) collective-permute-start(f32[2,2,16,1024]{3,2,1,0:T(8,128)S(1)} %get-tuple-element.783), channel_id=1, source_target_pairs={{2,0},{4,2},{6,4},{3,1},{5,3},{7,5},{10,8},{12,10},{14,12},{11,9},... | collective-permute-start | bytes 786440 | tf_op jit(solution)/shard_map/while/body/eval_jaxpr/ppermute | solution.py:21
  127.6 9.0 %collective-permute-start.3 = (f32[2,2,16,1024]{3,2,1,0:T(8,128)S(1)}, f32[2,2,16,1024]{3,2,1,0:T(8,128)S(1)}, u32[]{:S(2)}, u32[]{:S(2)}) collective-permute-start(f32[2,2,16,1024]{3,2,1,0:T(8,128)S(1)} %get-tuple-element.784), channel_id=1, source_target_pairs={{0,2},{2,4},{4,6},{1,3},{3,5},{5,7},{8,10},{10,12},{12,14},{9,11},... | collective-permute-start | bytes 786440 | tf_op jit(solution)/shard_map/while/body/eval_jaxpr/ppermute | solution.py:18
  141.5 10.3 %collective-permute-start.2 = (f32[2,2,16,1024]{3,2,1,0:T(8,128)S(1)}, f32[2,2,16,1024]{3,2,1,0:T(8,128)S(1)}, u32[]{:S(2)}, u32[]{:S(2)}) collective-permute-start(f32[2,2,16,1024]{3,2,1,0:T(8,128)S(1)} %get-tuple-element.783), channel_id=1, source_target_pairs={{2,0},{4,2},{6,4},{3,1},{5,3},{7,5},{10,8},{12,10},{14,12},{11,9},... | collective-permute-start | bytes 786440 | tf_op jit(solution)/shard_map/while/body/eval_jaxpr/ppermute | solution.py:21
  142.8 9.0 %collective-permute-start.3 = (f32[2,2,16,1024]{3,2,1,0:T(8,128)S(1)}, f32[2,2,16,1024]{3,2,1,0:T(8,128)S(1)}, u32[]{:S(2)}, u32[]{:S(2)}) collective-permute-start(f32[2,2,16,1024]{3,2,1,0:T(8,128)S(1)} %get-tuple-element.784), channel_id=1, source_target_pairs={{0,2},{2,4},{4,6},{1,3},{3,5},{5,7},{8,10},{10,12},{12,14},{9,11},... | collective-permute-start | bytes 786440 | tf_op jit(solution)/shard_map/while/body/eval_jaxpr/ppermute | solution.py:18
  156.7 10.3 %collective-permute-start.2 = (f32[2,2,16,1024]{3,2,1,0:T(8,128)S(1)}, f32[2,2,16,1024]{3,2,1,0:T(8,128)S(1)}, u32[]{:S(2)}, u32[]{:S(2)}) collective-permute-start(f32[2,2,16,1024]{3,2,1,0:T(8,128)S(1)} %get-tuple-element.783), channel_id=1, source_target_pairs={{2,0},{4,2},{6,4},{3,1},{5,3},{7,5},{10,8},{12,10},{14,12},{11,9},... | collective-permute-start | bytes 786440 | tf_op jit(solution)/shard_map/while/body/eval_jaxpr/ppermute | solution.py:21
  158.0 9.0 %collective-permute-start.3 = (f32[2,2,16,1024]{3,2,1,0:T(8,128)S(1)}, f32[2,2,16,1024]{3,2,1,0:T(8,128)S(1)}, u32[]{:S(2)}, u32[]{:S(2)}) collective-permute-start(f32[2,2,16,1024]{3,2,1,0:T(8,128)S(1)} %get-tuple-element.784), channel_id=1, source_target_pairs={{0,2},{2,4},{4,6},{1,3},{3,5},{5,7},{8,10},{10,12},{12,14},{9,11},... | collective-permute-start | bytes 786440 | tf_op jit(solution)/shard_map/while/body/eval_jaxpr/ppermute | solution.py:18
  192.3 81.2 %copy-start.39 = (f32[1,32,128]{2,1,0:T(8,128)S(1)}, f32[1,32,128]{2,1,0:T(8,128)}, u32[]{:S(2)}) copy-start(f32[1,32,128]{2,1,0:T(8,128)} %get-tuple-element.589) | copy-start | bytes 49156
  192.3 81.2 %copy-start.40 = (f32[1,32,128]{2,1,0:T(8,128)S(1)}, f32[1,32,128]{2,1,0:T(8,128)}, u32[]{:S(2)}) copy-start(f32[1,32,128]{2,1,0:T(8,128)} %get-tuple-element.590) | copy-start | bytes 49156
  248.3 5.4 %collective-permute-start.6 = (f32[2,1,128]{2,1,0:T(1,128)S(1)}, f32[2,1,128]{2,1,0:T(1,128)S(1)}, u32[]{:S(2)}, u32[]{:S(2)}) collective-permute-start(f32[2,1,128]{2,1,0:T(1,128)S(1)} %get-tuple-element.583), channel_id=1, source_target_pairs={{0,2},{2,4},{4,6},{1,3},{3,5},{5,7},{8,10},{10,12},{12,14},{9,11},... | collective-permute-start | bytes 3080 | tf_op jit(solution)/shard_map/ppermute | solution.py:18
  251.7 5.5 %collective-permute-start.7 = (f32[2,1,128]{2,1,0:T(1,128)S(1)}, f32[2,1,128]{2,1,0:T(1,128)S(1)}, u32[]{:S(2)}, u32[]{:S(2)}) collective-permute-start(f32[2,1,128]{2,1,0:T(1,128)S(1)} %get-tuple-element.584), channel_id=1, source_target_pairs={{2,0},{4,2},{6,4},{3,1},{5,3},{7,5},{10,8},{12,10},{14,12},{11,9},... | collective-permute-start | bytes 3080 | tf_op jit(solution)/shard_map/ppermute | solution.py:21
  257.2 5.9 %collective-permute-start.9 = (f32[2,34,1]{2,1,0:T(8,128)S(1)}, f32[2,34,1]{2,1,0:T(8,128)S(1)}, u32[]{:S(2)}, u32[]{:S(2)}) collective-permute-start(f32[2,34,1]{2,1,0:T(8,128)S(1)} %get-tuple-element.577), channel_id=1, source_target_pairs={{1,0},{8,1},{9,8},{16,9},{17,16},{24,17},{25,24},{3,2},{10,3},{11,... | collective-permute-start | bytes 824 | tf_op jit(solution)/shard_map/ppermute | solution.py:21
  258.5 6.2 %collective-permute-start.8 = (f32[2,34,1]{2,1,0:T(8,128)S(1)}, f32[2,34,1]{2,1,0:T(8,128)S(1)}, u32[]{:S(2)}, u32[]{:S(2)}) collective-permute-start(f32[2,34,1]{2,1,0:T(8,128)S(1)} %get-tuple-element.578), channel_id=1, source_target_pairs={{0,1},{1,8},{8,9},{9,16},{16,17},{17,24},{24,25},{2,3},{3,10},{10,... | collective-permute-start | bytes 824 | tf_op jit(solution)/shard_map/ppermute | solution.py:18
  266.9 13.5 %collective-permute-start.11 = (f32[32,1,128]{2,0,1:T(8,128)}, f32[32,1,128]{2,0,1:T(8,128)S(1)}, u32[]{:S(2)}, u32[]{:S(2)}) collective-permute-start(f32[32,1,128]{2,0,1:T(8,128)} %bitcast.93), channel_id=1, source_target_pairs={{2,0},{4,2},{6,4},{3,1},{5,3},{7,5},{10,8},{12,10},{14,12},{11,9},... | collective-permute-start | bytes 49160 | tf_op jit(solution)/shard_map/ppermute | solution.py:21
  268.2 8.6 %collective-permute-start.10 = (f32[32,1,128]{2,0,1:T(8,128)}, f32[32,1,128]{2,0,1:T(8,128)}, u32[]{:S(2)}, u32[]{:S(2)}) collective-permute-start(f32[32,1,128]{2,0,1:T(8,128)} %bitcast.92), channel_id=1, source_target_pairs={{0,2},{2,4},{4,6},{1,3},{3,5},{5,7},{8,10},{10,12},{12,14},{9,11},... | collective-permute-start | bytes 49160 | tf_op jit(solution)/shard_map/ppermute | solution.py:18
  284.3 8.7 %collective-permute-start.13 = (f32[32,34,1]{1,0,2:T(8,128)S(1)}, f32[32,34,1]{1,0,2:T(8,128)S(1)}, u32[]{:S(2)}, u32[]{:S(2)}) collective-permute-start(f32[32,34,1]{1,0,2:T(8,128)S(1)} %get-tuple-element.531), channel_id=1, source_target_pairs={{1,0},{8,1},{9,8},{16,9},{17,16},{24,17},{25,24},{3,2},{10,3},{11,... | collective-permute-start | bytes 13064 | tf_op jit(solution)/shard_map/ppermute | solution.py:21
  285.7 7.2 %collective-permute-start.12 = (f32[32,34,1]{1,0,2:T(8,128)S(1)}, f32[32,34,1]{1,0,2:T(8,128)S(1)}, u32[]{:S(2)}, u32[]{:S(2)}) collective-permute-start(f32[32,34,1]{1,0,2:T(8,128)S(1)} %get-tuple-element.532), channel_id=1, source_target_pairs={{0,1},{1,8},{8,9},{9,16},{16,17},{17,24},{24,25},{2,3},{3,10},{10,... | collective-permute-start | bytes 13064 | tf_op jit(solution)/shard_map/ppermute | solution.py:18
  343.1 22.8 %collective-permute-start.15 = (f32[32,1,128]{2,0,1:T(8,128)}, f32[32,1,128]{2,0,1:T(8,128)S(1)}, u32[]{:S(2)}, u32[]{:S(2)}) collective-permute-start(f32[32,1,128]{2,0,1:T(8,128)} %bitcast.95), channel_id=1, source_target_pairs={{2,0},{4,2},{6,4},{3,1},{5,3},{7,5},{10,8},{12,10},{14,12},{11,9},... | collective-permute-start | bytes 49160 | tf_op jit(solution)/shard_map/ppermute | solution.py:21
  344.4 17.9 %collective-permute-start.14 = (f32[32,1,128]{2,0,1:T(8,128)}, f32[32,1,128]{2,0,1:T(8,128)}, u32[]{:S(2)}, u32[]{:S(2)}) collective-permute-start(f32[32,1,128]{2,0,1:T(8,128)} %bitcast.94), channel_id=1, source_target_pairs={{0,2},{2,4},{4,6},{1,3},{3,5},{5,7},{8,10},{10,12},{12,14},{9,11},... | collective-permute-start | bytes 49160 | tf_op jit(solution)/shard_map/ppermute | solution.py:18
  355.8 14.4 %copy-start.6 = (f32[32,32,128]{1,0,2:T(8,128)}, f32[32,32,128]{1,0,2:T(8,128)S(1)}, u32[]{:S(2)}) copy-start(f32[32,32,128]{1,0,2:T(8,128)S(1)} %copy.139) | copy-start | bytes 1572868
  355.9 24.5 %collective-permute-start.23 = (f32[32,1,128]{2,0,1:T(8,128)}, f32[32,1,128]{2,0,1:T(8,128)}, u32[]{:S(2)}, u32[]{:S(2)}) collective-permute-start(f32[32,1,128]{2,0,1:T(8,128)} %bitcast.436), channel_id=1, source_target_pairs={{2,0},{4,2},{6,4},{3,1},{5,3},{7,5},{10,8},{12,10},{14,12},{11,9},... | collective-permute-start | bytes 49160 | tf_op jit(solution)/shard_map/ppermute | solution.py:21
  357.2 19.7 %collective-permute-start.22 = (f32[32,1,128]{2,0,1:T(8,128)}, f32[32,1,128]{2,0,1:T(8,128)}, u32[]{:S(2)}, u32[]{:S(2)}) collective-permute-start(f32[32,1,128]{2,0,1:T(8,128)} %bitcast.437), channel_id=1, source_target_pairs={{0,2},{2,4},{4,6},{1,3},{3,5},{5,7},{8,10},{10,12},{12,14},{9,11},... | collective-permute-start | bytes 49160 | tf_op jit(solution)/shard_map/ppermute | solution.py:18
  370.3 13.7 %copy-start.7 = (f32[32,32,128]{1,0,2:T(8,128)S(1)}, f32[32,32,128]{1,0,2:T(8,128)}, u32[]{:S(2)}) copy-start(f32[32,32,128]{1,0,2:T(8,128)} %copy.152) | copy-start | bytes 1572868
  370.3 40.7 %collective-permute-start.17 = (f32[32,34,1]{1,0,2:T(8,128)}, f32[32,34,1]{1,0,2:T(8,128)}, u32[]{:S(2)}, u32[]{:S(2)}) collective-permute-start(f32[32,34,1]{1,0,2:T(8,128)} %get-tuple-element.527), channel_id=1, source_target_pairs={{1,0},{8,1},{9,8},{16,9},{17,16},{24,17},{25,24},{3,2},{10,3},{11,... | collective-permute-start | bytes 13064 | tf_op jit(solution)/shard_map/ppermute | solution.py:21
  371.7 39.3 %collective-permute-start.16 = (f32[32,34,1]{1,0,2:T(8,128)}, f32[32,34,1]{1,0,2:T(8,128)}, u32[]{:S(2)}, u32[]{:S(2)}) collective-permute-start(f32[32,34,1]{1,0,2:T(8,128)} %get-tuple-element.528), channel_id=1, source_target_pairs={{0,1},{1,8},{8,9},{9,16},{16,17},{17,24},{24,25},{2,3},{3,10},{10,... | collective-permute-start | bytes 13064 | tf_op jit(solution)/shard_map/ppermute | solution.py:18
  385.0 10.1 %collective-permute-start.25 = (f32[32,34,1]{1,0,2:T(8,128)S(1)}, f32[32,34,1]{1,0,2:T(8,128)S(1)}, u32[]{:S(2)}, u32[]{:S(2)}) collective-permute-start(f32[32,34,1]{1,0,2:T(8,128)S(1)} %get-tuple-element.523), channel_id=1, source_target_pairs={{1,0},{8,1},{9,8},{16,9},{17,16},{24,17},{25,24},{3,2},{10,3},{11,... | collective-permute-start | bytes 13064 | tf_op jit(solution)/shard_map/ppermute | solution.py:21
  386.5 8.7 %collective-permute-start.24 = (f32[32,34,1]{1,0,2:T(8,128)S(1)}, f32[32,34,1]{1,0,2:T(8,128)S(1)}, u32[]{:S(2)}, u32[]{:S(2)}) collective-permute-start(f32[32,34,1]{1,0,2:T(8,128)S(1)} %get-tuple-element.524), channel_id=1, source_target_pairs={{0,1},{1,8},{8,9},{9,16},{16,17},{17,24},{24,25},{2,3},{3,10},{10,... | collective-permute-start | bytes 13064 | tf_op jit(solution)/shard_map/ppermute | solution.py:18
  480.0 47.3 %copy-start.1 = (f32[32,18]{0,1:T(8,128)S(1)}, f32[32,18]{0,1:T(8,128)}, u32[]{:S(2)}) copy-start(f32[32,18]{0,1:T(8,128)} %param.30) | copy-start | bytes 6916
  (37 other events, 246.9 us)
Sparse Core Ops, SparseCore 0:
  192.4 55.0 all-reduce.10
where the time goes:
time: 544 us; the launch traced here: 534 us
  local copies, waits for them, and re-layouts  169 us (31%)
  starting transfers between devices  117 us (22%)
  other arithmetic  78.2 us (14%)
  waiting for transfers between devices  76.8 us (14%)
  blocking collectives  39.2 us (7%)
  matrix products  37.4 us (7%)
  between operations  15.3 us (3%)
    ppermute x19, starting transfers between devices, extended_2(): lax.ppermute(lax.slice_in_dim(block, block.shape[dim] - width, None, axis...  91.8 us
    slice x25, local copies, waits for them, and re-layouts, patches(): extended[:, down:down + height, across:across + breadth]  83.9 us
    psum x1, waiting for transfers between devices, on_device(): gathered = lax.psum(imaging, ('shot', 'net'))  55.1 us
    psum x1, blocking collectives, on_device(): totals = lax.psum((grad_in, grad_mid, grad_out), ('shot', 'band', 'net'))  39.2 us
    concatenate x23, other arithmetic, extended_2(): block = jnp.concatenate([low, block, high], axis=dim)  27.2 us
    ppermute x19, starting transfers between devices, extended_2(): lax.ppermute(lax.slice_in_dim(block, 0, width, axis=dim), axis, backward)  24.9 us
    unnamed x126, local copies, waits for them, and re-layouts  22.8 us
    add x24, other arithmetic, block(): 2.0 * current[:, 4:-4] - earlier[:, 4:-4] + speed_part * laplace(current)  21.6 us
  transfers between devices with their start and end apart: 39, of which 11 were waited for; matrix products, arithmetic and copies ran while one was open for 28% of the time, Pallas kernels for 0%

commit v1 on v0

--- a/solution.py
+++ b/solution.py
@@ -163,7 +163,7 @@
     imaging = jnp.sum(stored * adjoint[::-1], axis=(0, 1))
     group_count = shot_here * lax.axis_size(("shot", "net"))
     start_col = lax.axis_index(("shot", "net")) * piece_cols
-    gathered = lax.psum(imaging, ("shot", "net"))
+    gathered = jnp.sum(lax.all_gather(imaging, ("shot", "net")), axis=0)
     summed = lax.dynamic_slice_in_dim(gathered, start_col, piece_cols, 1)
     scaled = summed / float(num_steps * group_count) ** 0.5
     velocity_piece = lax.dynamic_slice_in_dim(velocity, start_col, piece_cols, 1)

time: 544 us -> 495 us (0.910)
  waiting for transfers between devices: 76.8 us -> 33.6 us
    psum x1 -> x0, waiting for transfers between devices: 55.1 us -> none  [on_device(): gathered = lax.psum(imaging, ('shot', 'net'))]
    all_gather x0 -> x1, waiting for transfers between devices: none -> 9.1 us  [on_device(): gathered = jnp.sum(lax.all_gather(imaging, ('shot', 'net')), axis=0)]
  transfers between devices with their start and end apart: 39 -> 39, of which waited for: 11 -> 14; matrix products, arithmetic and copies ran while one was open for 28% -> 16% of each run, Pallas kernels for 0% -> 0%
where the time goes in v1:
time: 495 us; the launch traced here: 486 us
  local copies, waits for them, and re-layouts  167 us (34%)
  starting transfers between devices  115 us (23%)
  other arithmetic  75.4 us (15%)
  blocking collectives  39.3 us (8%)
  matrix products  37.4 us (8%)
  waiting for transfers between devices  33.6 us (7%)
  between operations  15.3 us (3%)
    ppermute x19, starting transfers between devices, extended_2(): lax.ppermute(lax.slice_in_dim(block, block.shape[dim] - width, None, axis...  90.5 us
    slice x25, local copies, waits for them, and re-layouts, patches(): extended[:, down:down + height, across:across + breadth]  83.9 us
    psum x1, blocking collectives, on_device(): totals = lax.psum((grad_in, grad_mid, grad_out), ('shot', 'band', 'net'))  39.3 us
    concatenate x23, other arithmetic, extended_2(): block = jnp.concatenate([low, block, high], axis=dim)  25.1 us
    ppermute x19, starting transfers between devices, extended_2(): lax.ppermute(lax.slice_in_dim(block, 0, width, axis=dim), axis, backward)  24.9 us
    unnamed x126, local copies, waits for them, and re-layouts  22 us
    add x24, other arithmetic, block(): 2.0 * current[:, 4:-4] - earlier[:, 4:-4] + speed_part * laplace(current)  21.6 us
    dot_general x16, matrix products, receiver_term(): injected = jnp.einsum('swk,sk->sw', table, residual, precision=highest)  16.8 us
  transfers between devices with their start and end apart: 39, of which 14 were waited for; matrix products, arithmetic and copies ran while one was open for 16% of the time, Pallas kernels for 0%

profile of v1, /device:TPU:0, one launch (start us, length us, event | category | flops | bytes accessed | tf_op | source)
XLA Modules:
  0.0 485.8 jit_solution(230208720382711872)
XLA Ops:
  8.2 5.0 %collective-permute-start.4 = (f32[16,1024]{1,0:T(8,128)S(1)}, f32[16,1024]{1,0:T(8,128)S(1)}, u32[]{:S(2)}, u32[]{:S(2)}) collective-permute-start(f32[16,1024]{1,0:T(8,128)S(1)} %get-tuple-element.563), channel_id=1, source_target_pairs={{0,2},{2,4},{4,6},{1,3},{3,5},{5,7},{8,10},{10,12},{12,14},{9,11},... | collective-permute-start | bytes 196616 | tf_op jit(solution)/shard_map/ppermute | solution.py:18
  22.0 60.4 %while.34 = (s32[]{:T(128)}, f32[2,32,1024]{2,1,0:T(8,128)S(1)}, f32[2,32,1024]{2,1,0:T(8,128)S(1)}, f32[4,4,2,32,1024]{4,3,2,1,0:T(8,128)}, f32[64,1024]{1,0:T(...) while((s32[]{:T(128)}, f32[2,32,1024]{2,1,0:T(8,128)S(1)}, ...), condition=%wide.region_1.2_spmd.clone, body=%wide.region_0.1_spmd.clone.sunk | while | flops 11801106 | bytes 31434516 | solution.py:156
  23.4 4.6 collective-permute-start.1
  38.5 5.0 %collective-permute-start.1 = (f32[2,2,16,1024]{3,2,1,0:T(8,128)S(1)}, f32[2,2,16,1024]{3,2,1,0:T(8,128)S(1)}, u32[]{:S(2)}, u32[]{:S(2)}) collective-permute-start(f32[2,2,16,1024]{3,2,1,0:T(8,128)S(1)} %get-tuple-element.761), channel_id=1, source_target_pairs={{0,2},{2,4},{4,6},{1,3},{3,5},{5,7},{8,10},{10,12},{12,14},{9,11},... | collective-permute-start | bytes 786440 | tf_op jit(solution)/shard_map/while/body/eval_jaxpr/ppermute | solution.py:18
  53.6 5.0 %collective-permute-start.1 = (f32[2,2,16,1024]{3,2,1,0:T(8,128)S(1)}, f32[2,2,16,1024]{3,2,1,0:T(8,128)S(1)}, u32[]{:S(2)}, u32[]{:S(2)}) collective-permute-start(f32[2,2,16,1024]{3,2,1,0:T(8,128)S(1)} %get-tuple-element.761), channel_id=1, source_target_pairs={{0,2},{2,4},{4,6},{1,3},{3,5},{5,7},{8,10},{10,12},{12,14},{9,11},... | collective-permute-start | bytes 786440 | tf_op jit(solution)/shard_map/while/body/eval_jaxpr/ppermute | solution.py:18
  68.7 5.0 %collective-permute-start.1 = (f32[2,2,16,1024]{3,2,1,0:T(8,128)S(1)}, f32[2,2,16,1024]{3,2,1,0:T(8,128)S(1)}, u32[]{:S(2)}, u32[]{:S(2)}) collective-permute-start(f32[2,2,16,1024]{3,2,1,0:T(8,128)S(1)} %get-tuple-element.761), channel_id=1, source_target_pairs={{0,2},{2,4},{4,6},{1,3},{3,5},{5,7},{8,10},{10,12},{12,14},{9,11},... | collective-permute-start | bytes 786440 | tf_op jit(solution)/shard_map/while/body/eval_jaxpr/ppermute | solution.py:18
  82.4 4.6 copy.175
  90.1 61.6 %while.35 = (s32[]{:T(128)}, f32[2,32,1024]{2,1,0:T(8,128)S(1)}, f32[2,32,1024]{2,1,0:T(8,128)S(1)}, f32[4,4,2,32,1024]{4,3,2,1,0:T(8,128)}, f32[64,1024]{1,0:T(...) while((s32[]{:T(128)}, f32[2,32,1024]{2,1,0:T(8,128)S(1)}, ...), condition=%wide.region_3.4_spmd.clone, body=%wide.region_2.3_spmd.clone.sunk | while | flops 27165204 | bytes 31534800 | solution.py:156
  91.9 5.0 %collective-permute-start.3 = (f32[2,2,16,1024]{3,2,1,0:T(8,128)S(1)}, f32[2,2,16,1024]{3,2,1,0:T(8,128)S(1)}, u32[]{:S(2)}, u32[]{:S(2)}) collective-permute-start(f32[2,2,16,1024]{3,2,1,0:T(8,128)S(1)} %get-tuple-element.784), channel_id=1, source_target_pairs={{0,2},{2,4},{4,6},{1,3},{3,5},{5,7},{8,10},{10,12},{12,14},{9,11},... | collective-permute-start | bytes 786440 | tf_op jit(solution)/shard_map/while/body/eval_jaxpr/ppermute | solution.py:18
  107.5 4.6 collective-permute-start.3
  122.7 4.6 collective-permute-start.3
  137.9 4.6 collective-permute-start.3
  151.7 6.6 %copy.176 = f32[16,2,32,1024]{3,0,1,2:T(8,128)} copy(f32[16,2,32,1024]{3,2,1,0:T(8,128)} %bitcast.369) | data formatting | bytes 8388608 | tf_op jit(solution)/shard_map/reshape | solution.py:157
  158.3 6.8 %rev.13 = f32[16,2,32,1024]{3,0,1,2:T(8,128)} reverse(f32[16,2,32,1024]{3,0,1,2:T(8,128)} %copy.176), dimensions={0} | reverse | bytes 8388608 | tf_op jit(solution)/shard_map/rev | solution.py:163
  165.2 7.0 %multiply_reduce_fusion = f32[32,1024]{1,0:T(8,128)} fusion(f32[16,2,32,1024]{3,0,1,2:T(8,128)} %rev.13, f32[16,2,32,1024]{3,2,1,0:T(8,128)} %bitcast.368), kind=kLoop, calls=%fused_computation.332 | loop fusion | flops 2064384 | bytes 8519680 | tf_op jit(solution)/shard_map/reduce_sum | solution.py:163
  172.3 3.9 collective-permute-start.18
  183.0 4.5 collective-permute-start.20
  189.1 9.1 %all-gather.3.cloned.1.call-done = f32[256,1024]{1,0:T(8,128)} async-done(((f32[32,1024]{1,0:T(8,128)}), f32[256,1024]{1,0:T(8,128)}) %all-gather.3.cloned.1.call-update) | async-done | bytes 1048592 | tf_op jit(solution)/shard_map/all_gather | solution.py:166
  204.3 4.1 collective-permute-done.7
  209.8 4.5 collective-permute-start.8
  219.5 5.1 %collective-permute-start.10 = (f32[32,1,128]{2,0,1:T(8,128)}, f32[32,1,128]{2,0,1:T(8,128)}, u32[]{:S(2)}, u32[]{:S(2)}) collective-permute-start(f32[32,1,128]{2,0,1:T(8,128)} %bitcast.93), channel_id=1, source_target_pairs={{0,2},{2,4},{4,6},{1,3},{3,5},{5,7},{8,10},{10,12},{12,14},{9,11},... | collective-permute-start | bytes 49160 | tf_op jit(solution)/shard_map/ppermute | solution.py:18
  228.1 3.6 copy.125
  237.0 5.3 %collective-permute-start.12 = (f32[32,34,1]{1,0,2:T(8,128)S(1)}, f32[32,34,1]{1,0,2:T(8,128)S(1)}, u32[]{:S(2)}, u32[]{:S(2)}) collective-permute-start(f32[32,34,1]{1,0,2:T(8,128)S(1)} %get-tuple-element.532), channel_id=1, source_target_pairs={{0,1},{1,8},{8,9},{9,16},{16,17},{17,24},{24,25},{2,3},{3,10},{10,... | collective-permute-start | bytes 13064 | tf_op jit(solution)/shard_map/ppermute | solution.py:18
  244.3 4.4 pad_maximum_fusion.4
  248.7 3.7 fusion.218
  252.5 3.5 copy.135
  262.9 3.8 fusion.219
  266.6 3.6 copy.133
  288.1 4.7 fusion.230
  295.7 5.1 %collective-permute-start.14 = (f32[32,1,128]{2,0,1:T(8,128)}, f32[32,1,128]{2,0,1:T(8,128)}, u32[]{:S(2)}, u32[]{:S(2)}) collective-permute-start(f32[32,1,128]{2,0,1:T(8,128)} %bitcast.95), channel_id=1, source_target_pairs={{0,2},{2,4},{4,6},{1,3},{3,5},{5,7},{8,10},{10,12},{12,14},{9,11},... | collective-permute-start | bytes 49160 | tf_op jit(solution)/shard_map/ppermute | solution.py:18
  308.4 5.1 %collective-permute-start.22 = (f32[32,1,128]{2,0,1:T(8,128)}, f32[32,1,128]{2,0,1:T(8,128)}, u32[]{:S(2)}, u32[]{:S(2)}) collective-permute-start(f32[32,1,128]{2,0,1:T(8,128)} %bitcast.439), channel_id=1, source_target_pairs={{0,2},{2,4},{4,6},{1,3},{3,5},{5,7},{8,10},{10,12},{12,14},{9,11},... | collective-permute-start | bytes 49160 | tf_op jit(solution)/shard_map/ppermute | solution.py:18
  313.6 3.6 copy.138
  323.0 5.1 %collective-permute-start.16 = (f32[32,34,1]{1,0,2:T(8,128)}, f32[32,34,1]{1,0,2:T(8,128)}, u32[]{:S(2)}, u32[]{:S(2)}) collective-permute-start(f32[32,34,1]{1,0,2:T(8,128)} %get-tuple-element.528), channel_id=1, source_target_pairs={{0,1},{1,8},{8,9},{9,16},{16,17},{17,24},{24,25},{2,3},{3,10},{10,... | collective-permute-start | bytes 13064 | tf_op jit(solution)/shard_map/ppermute | solution.py:18
  328.1 3.6 copy.151
  331.7 3.6 copy.153
  337.7 5.0 %collective-permute-start.24 = (f32[32,34,1]{1,0,2:T(8,128)S(1)}, f32[32,34,1]{1,0,2:T(8,128)S(1)}, u32[]{:S(2)}, u32[]{:S(2)}) collective-permute-start(f32[32,34,1]{1,0,2:T(8,128)S(1)} %get-tuple-element.524), channel_id=1, source_target_pairs={{0,1},{1,8},{8,9},{9,16},{16,17},{17,24},{24,25},{2,3},{3,10},{10,... | collective-permute-start | bytes 13064 | tf_op jit(solution)/shard_map/ppermute | solution.py:18
  346.5 3.6 pad_maximum_fusion.6
  362.2 7.1 %pad_maximum_fusion.5 = (f32[32,34,129]{1,0,2:T(8,128)S(1)}, f32[32,34,129]{1,0,2:T(8,128)S(1)}) fusion(f32[32,34,1]{1,0,2:T(8,128)} %collective-permute-done.17, f32[32,1,128]{1,0,2:T(8,128)} %copy.140, f32[32,32,128]{1,0,2:T(8,128)} %copy-done.6, f32[32,1,128]{1,0,2:T(8,128)} %copy.138, f32[32,34,1]{1,0,2:T(8,128)} %collective-permute-done.16), kind=kLoop, calls=%fused_computation.336 | loop fusion | flops 842112 | bytes 1688576 | tf_op jit(solution)/shard_map/concatenate | solution.py:22
  369.4 3.9 fusion.216
  376.7 3.6 copy.145
  383.8 6.7 %fusion.215 = (f32[32,32,128]{1,0,2:T(8,128)}, f32[32,32,128]{1,0,2:T(8,128)}, f32[32,32,128]{1,0,2:T(8,128)}) fusion(f32[32,34,129]{1,0,2:T(8,128)} %get-tuple-element.522), kind=kLoop, calls=%fused_computation.439 | loop fusion | bytes 3145728 | tf_op jit(solution)/shard_map/slice | solution.py:59
  394.0 3.5 copy.157
  397.6 3.5 copy.154
  412.6 3.8 fusion.217
  416.4 3.6 copy.146
  420.0 3.5 copy.144
  434.2 3.8 fusion.231
  439.4 39.3 %all-reduce.8 = (f32[32,18]{0,1:T(8,128)}, f32[32,288]{1,0:T(8,128)}, f32[1,288]{1,0:T(1,128)}) all-reduce(f32[32,18]{0,1:T(8,128)S(1)} %copy-done.40, f32[32,288]{1,0:T(8,128)S(1)} %copy-done.39, f32[1,288]{1,0:T(1,128)S(1)} %fusion.231), channel_id=1, replica_groups=mesh['shot'=4,'band'=4,'net'=2] {'shot','band','net'}, use_global_device_ids=true, to_apply=%region_6.7 | all-reduce | flops 10080 | bytes 80640 | tf_op jit(solution)/shard_map/psum | solution.py:191
  (472 shorter events, 219.1 us)
Async XLA Ops:
  7.2 209.5 %copy-start = (f32[32,18]{0,1:T(8,128)S(1)}, f32[32,18]{0,1:T(8,128)}, u32[]{:S(2)}) copy-start(f32[32,18]{0,1:T(8,128)} %param.30) | copy-start | bytes 6916
  7.2 14.8 %copy-start.3 = (f32[2,32,1024]{2,1,0:T(8,128)S(1)}, f32[2,32,1024]{2,1,0:T(8,128)}, u32[]{:S(2)}) copy-start(f32[2,32,1024]{2,1,0:T(8,128)} %param.20) | copy-start | bytes 786436
  7.2 14.8 %copy-start.4 = (f32[2,32,1024]{2,1,0:T(8,128)S(1)}, f32[2,32,1024]{2,1,0:T(8,128)}, u32[]{:S(2)}) copy-start(f32[2,32,1024]{2,1,0:T(8,128)} %param.21) | copy-start | bytes 786436
  7.2 14.8 %copy-start.41 = (s32[2]{0:T(128)S(1)}, s32[2]{0:T(128)}, u32[]{:S(2)}) copy-start(s32[2]{0:T(128)} %param.25) | copy-start | bytes 28
  7.2 191.0 %all-gather.3.cloned.1.call-start = ((), (), s32[]{:S(2)}) async-start(), calls=%async_computation | async-start | bytes 1179648 | tf_op jit(solution)/shard_map/all_gather | solution.py:166
  8.2 9.9 %collective-permute-start.4 = (f32[16,1024]{1,0:T(8,128)S(1)}, f32[16,1024]{1,0:T(8,128)S(1)}, u32[]{:S(2)}, u32[]{:S(2)}) collective-permute-start(f32[16,1024]{1,0:T(8,128)S(1)} %get-tuple-element.563), channel_id=1, source_target_pairs={{0,2},{2,4},{4,6},{1,3},{3,5},{5,7},{8,10},{10,12},{12,14},{9,11},... | collective-permute-start | bytes 196616 | tf_op jit(solution)/shard_map/ppermute | solution.py:18
  13.2 6.2 %collective-permute-start.5 = (f32[16,1024]{1,0:T(8,128)S(1)}, f32[16,1024]{1,0:T(8,128)S(1)}, u32[]{:S(2)}, u32[]{:S(2)}) collective-permute-start(f32[16,1024]{1,0:T(8,128)S(1)} %get-tuple-element.564), channel_id=1, source_target_pairs={{2,0},{4,2},{6,4},{3,1},{5,3},{7,5},{10,8},{12,10},{14,12},{11,9},... | collective-permute-start | bytes 196616 | tf_op jit(solution)/shard_map/ppermute | solution.py:21
  22.1 9.1 %collective-permute-start = (f32[2,2,16,1024]{3,2,1,0:T(8,128)S(1)}, f32[2,2,16,1024]{3,2,1,0:T(8,128)S(1)}, u32[]{:S(2)}, u32[]{:S(2)}) collective-permute-start(f32[2,2,16,1024]{3,2,1,0:T(8,128)S(1)} %get-tuple-element.760), channel_id=1, source_target_pairs={{2,0},{4,2},{6,4},{3,1},{5,3},{7,5},{10,8},{12,10},{14,12},{11,9},... | collective-permute-start | bytes 786440 | tf_op jit(solution)/shard_map/while/body/eval_jaxpr/ppermute | solution.py:21
  23.4 9.0 %collective-permute-start.1 = (f32[2,2,16,1024]{3,2,1,0:T(8,128)S(1)}, f32[2,2,16,1024]{3,2,1,0:T(8,128)S(1)}, u32[]{:S(2)}, u32[]{:S(2)}) collective-permute-start(f32[2,2,16,1024]{3,2,1,0:T(8,128)S(1)} %get-tuple-element.761), channel_id=1, source_target_pairs={{0,2},{2,4},{4,6},{1,3},{3,5},{5,7},{8,10},{10,12},{12,14},{9,11},... | collective-permute-start | bytes 786440 | tf_op jit(solution)/shard_map/while/body/eval_jaxpr/ppermute | solution.py:18
  37.2 8.7 %collective-permute-start = (f32[2,2,16,1024]{3,2,1,0:T(8,128)S(1)}, f32[2,2,16,1024]{3,2,1,0:T(8,128)S(1)}, u32[]{:S(2)}, u32[]{:S(2)}) collective-permute-start(f32[2,2,16,1024]{3,2,1,0:T(8,128)S(1)} %get-tuple-element.760), channel_id=1, source_target_pairs={{2,0},{4,2},{6,4},{3,1},{5,3},{7,5},{10,8},{12,10},{14,12},{11,9},... | collective-permute-start | bytes 786440 | tf_op jit(solution)/shard_map/while/body/eval_jaxpr/ppermute | solution.py:21
  38.5 8.9 %collective-permute-start.1 = (f32[2,2,16,1024]{3,2,1,0:T(8,128)S(1)}, f32[2,2,16,1024]{3,2,1,0:T(8,128)S(1)}, u32[]{:S(2)}, u32[]{:S(2)}) collective-permute-start(f32[2,2,16,1024]{3,2,1,0:T(8,128)S(1)} %get-tuple-element.761), channel_id=1, source_target_pairs={{0,2},{2,4},{4,6},{1,3},{3,5},{5,7},{8,10},{10,12},{12,14},{9,11},... | collective-permute-start | bytes 786440 | tf_op jit(solution)/shard_map/while/body/eval_jaxpr/ppermute | solution.py:18
  52.3 8.7 %collective-permute-start = (f32[2,2,16,1024]{3,2,1,0:T(8,128)S(1)}, f32[2,2,16,1024]{3,2,1,0:T(8,128)S(1)}, u32[]{:S(2)}, u32[]{:S(2)}) collective-permute-start(f32[2,2,16,1024]{3,2,1,0:T(8,128)S(1)} %get-tuple-element.760), channel_id=1, source_target_pairs={{2,0},{4,2},{6,4},{3,1},{5,3},{7,5},{10,8},{12,10},{14,12},{11,9},... | collective-permute-start | bytes 786440 | tf_op jit(solution)/shard_map/while/body/eval_jaxpr/ppermute | solution.py:21
  53.6 8.9 %collective-permute-start.1 = (f32[2,2,16,1024]{3,2,1,0:T(8,128)S(1)}, f32[2,2,16,1024]{3,2,1,0:T(8,128)S(1)}, u32[]{:S(2)}, u32[]{:S(2)}) collective-permute-start(f32[2,2,16,1024]{3,2,1,0:T(8,128)S(1)} %get-tuple-element.761), channel_id=1, source_target_pairs={{0,2},{2,4},{4,6},{1,3},{3,5},{5,7},{8,10},{10,12},{12,14},{9,11},... | collective-permute-start | bytes 786440 | tf_op jit(solution)/shard_map/while/body/eval_jaxpr/ppermute | solution.py:18
  67.4 8.7 %collective-permute-start = (f32[2,2,16,1024]{3,2,1,0:T(8,128)S(1)}, f32[2,2,16,1024]{3,2,1,0:T(8,128)S(1)}, u32[]{:S(2)}, u32[]{:S(2)}) collective-permute-start(f32[2,2,16,1024]{3,2,1,0:T(8,128)S(1)} %get-tuple-element.760), channel_id=1, source_target_pairs={{2,0},{4,2},{6,4},{3,1},{5,3},{7,5},{10,8},{12,10},{14,12},{11,9},... | collective-permute-start | bytes 786440 | tf_op jit(solution)/shard_map/while/body/eval_jaxpr/ppermute | solution.py:21
  68.7 8.9 %collective-permute-start.1 = (f32[2,2,16,1024]{3,2,1,0:T(8,128)S(1)}, f32[2,2,16,1024]{3,2,1,0:T(8,128)S(1)}, u32[]{:S(2)}, u32[]{:S(2)}) collective-permute-start(f32[2,2,16,1024]{3,2,1,0:T(8,128)S(1)} %get-tuple-element.761), channel_id=1, source_target_pairs={{0,2},{2,4},{4,6},{1,3},{3,5},{5,7},{8,10},{10,12},{12,14},{9,11},... | collective-permute-start | bytes 786440 | tf_op jit(solution)/shard_map/while/body/eval_jaxpr/ppermute | solution.py:18
  90.6 10.7 %collective-permute-start.2 = (f32[2,2,16,1024]{3,2,1,0:T(8,128)S(1)}, f32[2,2,16,1024]{3,2,1,0:T(8,128)S(1)}, u32[]{:S(2)}, u32[]{:S(2)}) collective-permute-start(f32[2,2,16,1024]{3,2,1,0:T(8,128)S(1)} %get-tuple-element.783), channel_id=1, source_target_pairs={{2,0},{4,2},{6,4},{3,1},{5,3},{7,5},{10,8},{12,10},{14,12},{11,9},... | collective-permute-start | bytes 786440 | tf_op jit(solution)/shard_map/while/body/eval_jaxpr/ppermute | solution.py:21
  91.9 9.5 %collective-permute-start.3 = (f32[2,2,16,1024]{3,2,1,0:T(8,128)S(1)}, f32[2,2,16,1024]{3,2,1,0:T(8,128)S(1)}, u32[]{:S(2)}, u32[]{:S(2)}) collective-permute-start(f32[2,2,16,1024]{3,2,1,0:T(8,128)S(1)} %get-tuple-element.784), channel_id=1, source_target_pairs={{0,2},{2,4},{4,6},{1,3},{3,5},{5,7},{8,10},{10,12},{12,14},{9,11},... | collective-permute-start | bytes 786440 | tf_op jit(solution)/shard_map/while/body/eval_jaxpr/ppermute | solution.py:18
  106.2 10.3 %collective-permute-start.2 = (f32[2,2,16,1024]{3,2,1,0:T(8,128)S(1)}, f32[2,2,16,1024]{3,2,1,0:T(8,128)S(1)}, u32[]{:S(2)}, u32[]{:S(2)}) collective-permute-start(f32[2,2,16,1024]{3,2,1,0:T(8,128)S(1)} %get-tuple-element.783), channel_id=1, source_target_pairs={{2,0},{4,2},{6,4},{3,1},{5,3},{7,5},{10,8},{12,10},{14,12},{11,9},... | collective-permute-start | bytes 786440 | tf_op jit(solution)/shard_map/while/body/eval_jaxpr/ppermute | solution.py:21
  107.5 9.0 %collective-permute-start.3 = (f32[2,2,16,1024]{3,2,1,0:T(8,128)S(1)}, f32[2,2,16,1024]{3,2,1,0:T(8,128)S(1)}, u32[]{:S(2)}, u32[]{:S(2)}) collective-permute-start(f32[2,2,16,1024]{3,2,1,0:T(8,128)S(1)} %get-tuple-element.784), channel_id=1, source_target_pairs={{0,2},{2,4},{4,6},{1,3},{3,5},{5,7},{8,10},{10,12},{12,14},{9,11},... | collective-permute-start | bytes 786440 | tf_op jit(solution)/shard_map/while/body/eval_jaxpr/ppermute | solution.py:18
  121.4 10.3 %collective-permute-start.2 = (f32[2,2,16,1024]{3,2,1,0:T(8,128)S(1)}, f32[2,2,16,1024]{3,2,1,0:T(8,128)S(1)}, u32[]{:S(2)}, u32[]{:S(2)}) collective-permute-start(f32[2,2,16,1024]{3,2,1,0:T(8,128)S(1)} %get-tuple-element.783), channel_id=1, source_target_pairs={{2,0},{4,2},{6,4},{3,1},{5,3},{7,5},{10,8},{12,10},{14,12},{11,9},... | collective-permute-start | bytes 786440 | tf_op jit(solution)/shard_map/while/body/eval_jaxpr/ppermute | solution.py:21
  122.7 9.0 %collective-permute-start.3 = (f32[2,2,16,1024]{3,2,1,0:T(8,128)S(1)}, f32[2,2,16,1024]{3,2,1,0:T(8,128)S(1)}, u32[]{:S(2)}, u32[]{:S(2)}) collective-permute-start(f32[2,2,16,1024]{3,2,1,0:T(8,128)S(1)} %get-tuple-element.784), channel_id=1, source_target_pairs={{0,2},{2,4},{4,6},{1,3},{3,5},{5,7},{8,10},{10,12},{12,14},{9,11},... | collective-permute-start | bytes 786440 | tf_op jit(solution)/shard_map/while/body/eval_jaxpr/ppermute | solution.py:18
  136.6 10.3 %collective-permute-start.2 = (f32[2,2,16,1024]{3,2,1,0:T(8,128)S(1)}, f32[2,2,16,1024]{3,2,1,0:T(8,128)S(1)}, u32[]{:S(2)}, u32[]{:S(2)}) collective-permute-start(f32[2,2,16,1024]{3,2,1,0:T(8,128)S(1)} %get-tuple-element.783), channel_id=1, source_target_pairs={{2,0},{4,2},{6,4},{3,1},{5,3},{7,5},{10,8},{12,10},{14,12},{11,9},... | collective-permute-start | bytes 786440 | tf_op jit(solution)/shard_map/while/body/eval_jaxpr/ppermute | solution.py:21
  137.9 9.0 %collective-permute-start.3 = (f32[2,2,16,1024]{3,2,1,0:T(8,128)S(1)}, f32[2,2,16,1024]{3,2,1,0:T(8,128)S(1)}, u32[]{:S(2)}, u32[]{:S(2)}) collective-permute-start(f32[2,2,16,1024]{3,2,1,0:T(8,128)S(1)} %get-tuple-element.784), channel_id=1, source_target_pairs={{0,2},{2,4},{4,6},{1,3},{3,5},{5,7},{8,10},{10,12},{12,14},{9,11},... | collective-permute-start | bytes 786440 | tf_op jit(solution)/shard_map/while/body/eval_jaxpr/ppermute | solution.py:18
  165.2 13.9 %copy-start.43 = (f32[1,288]{1,0:T(1,128)S(1)}, f32[1,288]{1,0:T(1,128)}, u32[]{:S(2)}) copy-start(f32[1,288]{1,0:T(1,128)} %param.32) | copy-start | bytes 3460
  172.3 8.3 %collective-permute-start.18 = (f32[1,1,128]{2,1,0:T(1,128)S(1)}, f32[1,1,128]{2,1,0:T(1,128)S(1)}, u32[]{:S(2)}, u32[]{:S(2)}) collective-permute-start(f32[1,1,128]{2,1,0:T(1,128)S(1)} %get-tuple-element.591), channel_id=1, source_target_pairs={{0,2},{2,4},{4,6},{1,3},{3,5},{5,7},{8,10},{10,12},{12,14},{9,11},... | collective-permute-start | bytes 1544 | tf_op jit(solution)/shard_map/ppermute | solution.py:18
  176.2 5.5 %collective-permute-start.19 = (f32[1,1,128]{2,1,0:T(1,128)S(1)}, f32[1,1,128]{2,1,0:T(1,128)S(1)}, u32[]{:S(2)}, u32[]{:S(2)}) collective-permute-start(f32[1,1,128]{2,1,0:T(1,128)S(1)} %get-tuple-element.592), channel_id=1, source_target_pairs={{2,0},{4,2},{6,4},{3,1},{5,3},{7,5},{10,8},{12,10},{14,12},{11,9},... | collective-permute-start | bytes 1544 | tf_op jit(solution)/shard_map/ppermute | solution.py:21
  181.7 5.9 %collective-permute-start.21 = (f32[1,34,1]{2,1,0:T(8,128)S(1)}, f32[1,34,1]{2,1,0:T(8,128)S(1)}, u32[]{:S(2)}, u32[]{:S(2)}) collective-permute-start(f32[1,34,1]{2,1,0:T(8,128)S(1)} %get-tuple-element.585), channel_id=1, source_target_pairs={{1,0},{8,1},{9,8},{16,9},{17,16},{24,17},{25,24},{3,2},{10,3},{11,... | collective-permute-start | bytes 416 | tf_op jit(solution)/shard_map/ppermute | solution.py:21
  183.0 6.0 %collective-permute-start.20 = (f32[1,34,1]{2,1,0:T(8,128)S(1)}, f32[1,34,1]{2,1,0:T(8,128)S(1)}, u32[]{:S(2)}, u32[]{:S(2)}) collective-permute-start(f32[1,34,1]{2,1,0:T(8,128)S(1)} %get-tuple-element.586), channel_id=1, source_target_pairs={{0,1},{1,8},{8,9},{9,16},{16,17},{17,24},{24,25},{2,3},{3,10},{10,... | collective-permute-start | bytes 416 | tf_op jit(solution)/shard_map/ppermute | solution.py:18
  199.6 4.7 collective-permute-start.6
  203.0 5.5 %collective-permute-start.7 = (f32[2,1,128]{2,1,0:T(1,128)S(1)}, f32[2,1,128]{2,1,0:T(1,128)S(1)}, u32[]{:S(2)}, u32[]{:S(2)}) collective-permute-start(f32[2,1,128]{2,1,0:T(1,128)S(1)} %get-tuple-element.584), channel_id=1, source_target_pairs={{2,0},{4,2},{6,4},{3,1},{5,3},{7,5},{10,8},{12,10},{14,12},{11,9},... | collective-permute-start | bytes 3080 | tf_op jit(solution)/shard_map/ppermute | solution.py:21
  208.5 5.9 %collective-permute-start.9 = (f32[2,34,1]{2,1,0:T(8,128)S(1)}, f32[2,34,1]{2,1,0:T(8,128)S(1)}, u32[]{:S(2)}, u32[]{:S(2)}) collective-permute-start(f32[2,34,1]{2,1,0:T(8,128)S(1)} %get-tuple-element.577), channel_id=1, source_target_pairs={{1,0},{8,1},{9,8},{16,9},{17,16},{24,17},{25,24},{3,2},{10,3},{11,... | collective-permute-start | bytes 824 | tf_op jit(solution)/shard_map/ppermute | solution.py:21
  209.8 6.2 %collective-permute-start.8 = (f32[2,34,1]{2,1,0:T(8,128)S(1)}, f32[2,34,1]{2,1,0:T(8,128)S(1)}, u32[]{:S(2)}, u32[]{:S(2)}) collective-permute-start(f32[2,34,1]{2,1,0:T(8,128)S(1)} %get-tuple-element.578), channel_id=1, source_target_pairs={{0,1},{1,8},{8,9},{9,16},{16,17},{17,24},{24,25},{2,3},{3,10},{10,... | collective-permute-start | bytes 824 | tf_op jit(solution)/shard_map/ppermute | solution.py:18
  218.2 13.5 %collective-permute-start.11 = (f32[32,1,128]{2,0,1:T(8,128)}, f32[32,1,128]{2,0,1:T(8,128)S(1)}, u32[]{:S(2)}, u32[]{:S(2)}) collective-permute-start(f32[32,1,128]{2,0,1:T(8,128)} %bitcast.94), channel_id=1, source_target_pairs={{2,0},{4,2},{6,4},{3,1},{5,3},{7,5},{10,8},{12,10},{14,12},{11,9},... | collective-permute-start | bytes 49160 | tf_op jit(solution)/shard_map/ppermute | solution.py:21
  219.5 8.6 %collective-permute-start.10 = (f32[32,1,128]{2,0,1:T(8,128)}, f32[32,1,128]{2,0,1:T(8,128)}, u32[]{:S(2)}, u32[]{:S(2)}) collective-permute-start(f32[32,1,128]{2,0,1:T(8,128)} %bitcast.93), channel_id=1, source_target_pairs={{0,2},{2,4},{4,6},{1,3},{3,5},{5,7},{8,10},{10,12},{12,14},{9,11},... | collective-permute-start | bytes 49160 | tf_op jit(solution)/shard_map/ppermute | solution.py:18
  235.6 8.7 %collective-permute-start.13 = (f32[32,34,1]{1,0,2:T(8,128)S(1)}, f32[32,34,1]{1,0,2:T(8,128)S(1)}, u32[]{:S(2)}, u32[]{:S(2)}) collective-permute-start(f32[32,34,1]{1,0,2:T(8,128)S(1)} %get-tuple-element.531), channel_id=1, source_target_pairs={{1,0},{8,1},{9,8},{16,9},{17,16},{24,17},{25,24},{3,2},{10,3},{11,... | collective-permute-start | bytes 13064 | tf_op jit(solution)/shard_map/ppermute | solution.py:21
  237.0 7.2 %collective-permute-start.12 = (f32[32,34,1]{1,0,2:T(8,128)S(1)}, f32[32,34,1]{1,0,2:T(8,128)S(1)}, u32[]{:S(2)}, u32[]{:S(2)}) collective-permute-start(f32[32,34,1]{1,0,2:T(8,128)S(1)} %get-tuple-element.532), channel_id=1, source_target_pairs={{0,1},{1,8},{8,9},{9,16},{16,17},{17,24},{24,25},{2,3},{3,10},{10,... | collective-permute-start | bytes 13064 | tf_op jit(solution)/shard_map/ppermute | solution.py:18
  294.4 22.8 %collective-permute-start.15 = (f32[32,1,128]{2,0,1:T(8,128)}, f32[32,1,128]{2,0,1:T(8,128)S(1)}, u32[]{:S(2)}, u32[]{:S(2)}) collective-permute-start(f32[32,1,128]{2,0,1:T(8,128)} %bitcast.96), channel_id=1, source_target_pairs={{2,0},{4,2},{6,4},{3,1},{5,3},{7,5},{10,8},{12,10},{14,12},{11,9},... | collective-permute-start | bytes 49160 | tf_op jit(solution)/shard_map/ppermute | solution.py:21
  295.7 17.9 %collective-permute-start.14 = (f32[32,1,128]{2,0,1:T(8,128)}, f32[32,1,128]{2,0,1:T(8,128)}, u32[]{:S(2)}, u32[]{:S(2)}) collective-permute-start(f32[32,1,128]{2,0,1:T(8,128)} %bitcast.95), channel_id=1, source_target_pairs={{0,2},{2,4},{4,6},{1,3},{3,5},{5,7},{8,10},{10,12},{12,14},{9,11},... | collective-permute-start | bytes 49160 | tf_op jit(solution)/shard_map/ppermute | solution.py:18
  307.1 14.4 %copy-start.6 = (f32[32,32,128]{1,0,2:T(8,128)}, f32[32,32,128]{1,0,2:T(8,128)S(1)}, u32[]{:S(2)}) copy-start(f32[32,32,128]{1,0,2:T(8,128)S(1)} %copy.139) | copy-start | bytes 1572868
  307.1 24.5 %collective-permute-start.23 = (f32[32,1,128]{2,0,1:T(8,128)}, f32[32,1,128]{2,0,1:T(8,128)}, u32[]{:S(2)}, u32[]{:S(2)}) collective-permute-start(f32[32,1,128]{2,0,1:T(8,128)} %bitcast.438), channel_id=1, source_target_pairs={{2,0},{4,2},{6,4},{3,1},{5,3},{7,5},{10,8},{12,10},{14,12},{11,9},... | collective-permute-start | bytes 49160 | tf_op jit(solution)/shard_map/ppermute | solution.py:21
  308.4 19.7 %collective-permute-start.22 = (f32[32,1,128]{2,0,1:T(8,128)}, f32[32,1,128]{2,0,1:T(8,128)}, u32[]{:S(2)}, u32[]{:S(2)}) collective-permute-start(f32[32,1,128]{2,0,1:T(8,128)} %bitcast.439), channel_id=1, source_target_pairs={{0,2},{2,4},{4,6},{1,3},{3,5},{5,7},{8,10},{10,12},{12,14},{9,11},... | collective-permute-start | bytes 49160 | tf_op jit(solution)/shard_map/ppermute | solution.py:18
  321.5 13.7 %copy-start.7 = (f32[32,32,128]{1,0,2:T(8,128)S(1)}, f32[32,32,128]{1,0,2:T(8,128)}, u32[]{:S(2)}) copy-start(f32[32,32,128]{1,0,2:T(8,128)} %copy.152) | copy-start | bytes 1572868
  321.5 40.7 %collective-permute-start.17 = (f32[32,34,1]{1,0,2:T(8,128)}, f32[32,34,1]{1,0,2:T(8,128)}, u32[]{:S(2)}, u32[]{:S(2)}) collective-permute-start(f32[32,34,1]{1,0,2:T(8,128)} %get-tuple-element.527), channel_id=1, source_target_pairs={{1,0},{8,1},{9,8},{16,9},{17,16},{24,17},{25,24},{3,2},{10,3},{11,... | collective-permute-start | bytes 13064 | tf_op jit(solution)/shard_map/ppermute | solution.py:21
  323.0 39.3 %collective-permute-start.16 = (f32[32,34,1]{1,0,2:T(8,128)}, f32[32,34,1]{1,0,2:T(8,128)}, u32[]{:S(2)}, u32[]{:S(2)}) collective-permute-start(f32[32,34,1]{1,0,2:T(8,128)} %get-tuple-element.528), channel_id=1, source_target_pairs={{0,1},{1,8},{8,9},{9,16},{16,17},{17,24},{24,25},{2,3},{3,10},{10,... | collective-permute-start | bytes 13064 | tf_op jit(solution)/shard_map/ppermute | solution.py:18
  336.3 10.1 %collective-permute-start.25 = (f32[32,34,1]{1,0,2:T(8,128)S(1)}, f32[32,34,1]{1,0,2:T(8,128)S(1)}, u32[]{:S(2)}, u32[]{:S(2)}) collective-permute-start(f32[32,34,1]{1,0,2:T(8,128)S(1)} %get-tuple-element.523), channel_id=1, source_target_pairs={{1,0},{8,1},{9,8},{16,9},{17,16},{24,17},{25,24},{3,2},{10,3},{11,... | collective-permute-start | bytes 13064 | tf_op jit(solution)/shard_map/ppermute | solution.py:21
  337.7 8.7 %collective-permute-start.24 = (f32[32,34,1]{1,0,2:T(8,128)S(1)}, f32[32,34,1]{1,0,2:T(8,128)S(1)}, u32[]{:S(2)}, u32[]{:S(2)}) collective-permute-start(f32[32,34,1]{1,0,2:T(8,128)S(1)} %get-tuple-element.524), channel_id=1, source_target_pairs={{0,1},{1,8},{8,9},{9,16},{16,17},{17,24},{24,25},{2,3},{3,10},{10,... | collective-permute-start | bytes 13064 | tf_op jit(solution)/shard_map/ppermute | solution.py:18
  394.0 12.6 %copy-start.20 = (f32[32,4096]{1,0:T(8,128)S(1)}, f32[32,4096]{1,0:T(8,128)}, u32[]{:S(2)}) copy-start(f32[32,4096]{1,0:T(8,128)} %copy-done.19) | copy-start | bytes 1572868
  431.3 47.4 %copy-start.1 = (f32[32,18]{0,1:T(8,128)S(1)}, f32[32,18]{0,1:T(8,128)}, u32[]{:S(2)}) copy-start(f32[32,18]{0,1:T(8,128)} %param.30) | copy-start | bytes 6916
  (37 other events, 246.5 us)
Sparse Core Ops, SparseCore 0:
  172.4 25.8 all-gather.2
